TPU v7x, 32 devices: a whole 2x2x4 slice. The times are simulated.
32 devices in a mesh: sub: 32 (over z, y, x, core).
Axes of the slice: x: 2, y: 2, z: 4, core: 2. Of those that a mesh axis runs over, the one named last changes fastest.
Arguments:
- images: float32 [2, 4, 512, 4096], P(None, None, 'sub'), may hold values from -6 to 6
- anchors: int32 [128], P('sub'), may hold values from 0 to 4095, as said below
- patches: int32 [128], P('sub'), may hold values from 0 to 31
- coeffs: float32 [4, 45, 32], P(None, None, 'sub'), may hold values from -1.2 to 1.2
- zbasis: float32 [45, 4096], replicated, may hold values from -4 to 4
Outputs:
- new_coeffs: float32 [4, 45, 32], P(None, None, 'sub')
- last_gradient: float32 [4, 45, 32], P(None, None, 'sub')
Inputs may be any that keep to these rules, and one draw needn't show every extreme that they name: `anchors`: the first column of subfield s lies among the 128 columns that begin at 128 * (s // 4).
All inputs are finite; a program needn't handle non-finite values.
Results may differ from a plain program's by a relative error of at most 0.0003.
Values sent between devices are 32-bit elements; how exact they have to be, the bound alone decides.
A program may use at most 128 MiB of HBM per device.

v0:
```python
import math
import jax
import jax.numpy as jnp
from jax import lax
from jax.sharding import PartitionSpec as P

SUB = 128
CH = 2
TR = 4
ITERS = 2
PUP = 64
GAMMA = 0.01
STEP_SIZE = 0.05


def from_behind(block, axis, distance):
    devices = range(lax.axis_size(axis))
    route = [(i - distance, i) for i in devices if i - distance in devices]
    return lax.ppermute(block, axis, route)


def taper(length):
    cells = jnp.arange(length, dtype=jnp.float32)
    return 0.5 - 0.5 * jnp.cos(2.0 * math.pi * (cells + 0.5) / length)


def aperture(width):
    centred = jnp.arange(width, dtype=jnp.float32) - width / 2 + 0.5
    radius = centred[:, None] ** 2 + centred[None, :] ** 2
    return (radius <= (width / 2) ** 2).astype(jnp.float32)


def dft_tables(length):
    indices = jnp.arange(length, dtype=jnp.int32)
    product_mod = indices[:, None] * indices[None, :] % length
    angles = 2.0 * math.pi / length * product_mod.astype(jnp.float32)
    return (jnp.cos(angles), -jnp.sin(angles))


def complex_dft(real_part, imag_part, left_table, right_table):
    highest = lax.Precision.HIGHEST
    right_real, right_imag = right_table
    left_real, left_imag = left_table
    half_real = jnp.einsum("...ab,kb->...ak", real_part, right_real, precision=highest)
    half_imag = jnp.einsum("...ab,kb->...ak", real_part, right_imag, precision=highest)
    if imag_part is not None:
        half_real = half_real - jnp.einsum(
            "...ab,kb->...ak", imag_part, right_imag, precision=highest
        )
        half_imag = half_imag + jnp.einsum(
            "...ab,kb->...ak", imag_part, right_real, precision=highest
        )
    out_real = jnp.einsum("ja,...ak->...jk", left_real, half_real, precision=highest) - jnp.einsum(
        "ja,...ak->...jk", left_imag, half_imag, precision=highest
    )
    out_imag = jnp.einsum("ja,...ak->...jk", left_real, half_imag, precision=highest) + jnp.einsum(
        "ja,...ak->...jk", left_imag, half_real, precision=highest
    )
    return (out_real, out_imag)


def on_device(images, anchors, patches, coeffs, zbasis):
    highest = lax.Precision.HIGHEST
    devices = lax.axis_size("sub")
    device_index = lax.axis_index("sub")
    strip_width = images.shape[3] // devices
    reach = SUB // strip_width
    column_strip = lax.all_to_all(images, "sub", split_axis=3, concat_axis=2, tiled=True)
    strip_list = [column_strip]
    for step_right in range(1, reach + 1):
        strip_list.append(from_behind(column_strip, "sub", -step_right))
    widened = jnp.concatenate(strip_list, axis=3)
    offsets = anchors - device_index * strip_width
    subfield_list = []
    for row_tile in range(TR):
        strip_rows = widened[:, :, row_tile * SUB : (row_tile + 1) * SUB, :]
        subfield_list.append(lax.dynamic_slice_in_dim(strip_rows, offsets[row_tile], SUB, 3))
    window_two = taper(SUB)[:, None] * taper(SUB)[None, :]
    subfields = jnp.stack(subfield_list, axis=2) * window_two
    full_real, full_imag = dft_tables(SUB)
    full_table = (full_real, full_imag)
    pupil_table = (full_real[:, :PUP], full_imag[:, :PUP])
    data_real, data_imag = complex_dft(subfields, None, full_table, full_table)
    power_sum = jnp.sum(data_real * data_real + data_imag * data_imag, axis=1)
    pupil_mask = aperture(PUP)
    pupil_area = jnp.sum(pupil_mask)
    ratios = 1.0 / (1.0 + 0.25 * jnp.arange(CH, dtype=jnp.float32))
    owned_count = coeffs.shape[2]
    total_patches = owned_count * devices
    selector = (patches[None, :] == jnp.arange(total_patches, dtype=jnp.int32)[:, None]).astype(
        jnp.float32
    )

    def objective(chosen):
        phases = jnp.einsum("fms,mq->fsq", chosen, zbasis, precision=highest)
        phases = phases.reshape(phases.shape[:2] + (PUP, PUP))
        scaled = ratios[:, None, None, None, None] * phases[None]
        pupil_real = pupil_mask * jnp.cos(scaled)
        pupil_imag = pupil_mask * jnp.sin(scaled)
        field_real, field_imag = complex_dft(pupil_real, pupil_imag, pupil_table, pupil_table)
        psf_values = (field_real * field_real + field_imag * field_imag) / (SUB * SUB * pupil_area)
        otf_real, otf_imag = complex_dft(psf_values, None, full_table, full_table)
        cross_real = jnp.sum(data_real * otf_real + data_imag * otf_imag, axis=1)
        cross_imag = jnp.sum(data_imag * otf_real - data_real * otf_imag, axis=1)
        denominator = jnp.sum(otf_real * otf_real + otf_imag * otf_imag, axis=1) + GAMMA
        return (
            jnp.sum(power_sum - (cross_real * cross_real + cross_imag * cross_imag) / denominator)
            / SUB**4
        )

    current = coeffs
    gradient = jnp.zeros_like(coeffs)
    for iteration in range(ITERS):
        gathered = lax.all_gather(current, "sub", axis=2, tiled=True)
        chosen = jnp.einsum("fmp,ps->fms", gathered, selector, precision=highest)
        loss_value, pullback = jax.vjp(objective, chosen)
        (slopes,) = pullback(jnp.ones_like(loss_value))
        spread = jnp.einsum("fms,ps->fmp", slopes, selector, precision=highest)
        gradient = lax.psum_scatter(spread, "sub", scatter_dimension=2, tiled=True)
        current = current - STEP_SIZE * gradient
    return (current, gradient)


def solution(mesh):
    return jax.shard_map(
        on_device,
        mesh=mesh,
        in_specs=(P(None, None, "sub", None), P("sub"), P("sub"), P(None, None, "sub"), P()),
        out_specs=(P(None, None, "sub"), P(None, None, "sub")),
        check_vma=False,
    )
```

profile of v0, /device:TPU:10, one launch (start us, length us, event | category | flops | bytes accessed | tf_op | source)
XLA Modules:
  0.0 485.6 jit_solution(7883281226299236298)
XLA Ops:
  0.6 13.1 %copy.172 = f32[2,4,16,4096]{2,1,0,3:T(4,128)} copy(f32[2,4,16,4096]{3,2,1,0:T(8,128)} %param.5) | data formatting | bytes 4194304 | tf_op args[0]
  13.7 16.4 %reshape.149 = f32[32,1,16384]{2,1,0:T(1,128)} reshape(f32[4096,2,4,16]{3,2,1,0:T(4,128)} %bitcast.273) | data formatting | bytes 4194304
  30.1 6.1 %all-to-all-start = ((f32[32,1,16384]{2,1,0:T(1,128)}), f32[32,1,16384]{2,1,0:T(1,128)}, u32[]{:S(2)}, u32[]{:S(2)}) async-start(f32[32,1,16384]{2,1,0:T(1,128)} %reshape.149), calls=%async_computation | async-start | bytes 4194304 | tf_op jit(solution)/shard_map/all_to_all | solution.py:68
  36.3 71.0 %all_gather.6 = f32[4,45,32]{1,0,2:T(4,128)S(1)} all-gather(f32[4,45,1]{1,0,2:T(4,128)S(1)} %bitcast.277), channel_id=1, replica_groups=mesh['sub'=32] {'sub'}, dimensions={2}, use_global_device_ids=true | all-gather | bytes 23760 | tf_op jit(solution)/shard_map/all_gather | solution.py:114
  111.0 4.4 fusion.52
  115.4 4.4 fusion.54
  119.8 4.6 fusion.63
  124.3 4.4 fusion.60
  128.7 3.4 fusion.348
  132.2 3.8 fusion.349
  136.0 3.5 convolution_subtract_fusion.1
  139.5 3.4 convolution_add_fusion.1
  144.3 4.0 fusion.14
  148.8 8.7 %reduce.6 = f32[32,16384]{1,0:T(8,128)} reduce(f32[32,1,16384]{2,1,0:T(1,128)} %all-to-all-done, f32[]{:T(128)} %broadcast.349), dimensions={1}, to_apply=%all_to_all.13.reduce_sub_computation | reduce | bytes 4194308 | tf_op jit(solution)/shard_map/all_to_all | solution.py:68
  157.6 14.7 %reshape.150 = f32[4096,2,4,16]{3,2,1,0:T(4,128)} reshape(f32[32,16384]{1,0:T(8,128)} %reduce.6) | data formatting | bytes 4194304
  172.3 13.7 %copy.286 = f32[2,4,16,32,128]{4,2,3,1,0:T(8,128)} copy(f32[2,4,16,32,128]{2,1,0,4,3:T(4,128)} %bitcast.272) | data formatting | bytes 4194304 | tf_op jit(solution)/shard_map/all_to_all | solution.py:68
  186.0 3.1 collective-permute-start
  197.3 3.8 fusion.169
  201.1 2.5 fusion.12
  210.2 2.6 collective-permute-done
  217.2 2.4 fusion.99
  219.6 2.4 fusion.98
  228.2 2.9 subtract_reduce_fusion.1
  239.3 2.3 fusion.30
  241.6 3.6 fusion.8
  245.2 4.9 %add_divide_fusion.2 = f32[2,4,4,128,128]{4,3,2,1,0:T(8,128)} fusion(f32[2,4,4,128,128]{4,3,2,1,0:T(8,128)S(1)} %fusion.8, f32[2,4,4,128,128]{4,3,2,1,0:T(8,128)S(1)} %fusion.159, f32[2,4,4,128,128]{4,3,2,1,0:T(8,128)S(1)} %fusion.30, f32[]{:T(128)S(6)} %mul.931), kind=kOutput, calls=%fused_computation.48 | convolution fusion | flops 807124992 | bytes 8388612 | tf_op jit(solution)/shard_map/transpose(jvp(...ab,kb->...ak))/dot_general | solution.py:45
  250.1 3.4 copy.193
  253.5 4.9 %fusion.104 = f32[2,4,4,128,64]{3,4,2,1,0:T(8,128)S(1)} fusion(f32[2,4,4,128,128]{3,4,2,1,0:T(8,128)} %copy.193, f32[2,4,4,128,128]{4,3,2,1,0:T(8,128)} %copy-done.7, f32[128,128]{0,1:T(8,128)S(1)} %sine_negate_fusion), kind=kOutput, calls=%fused_computation.126 | convolution fusion | flops 403701760 | bytes 5275648 | tf_op jit(solution)/shard_map/transpose(jvp(ja,...ak->...jk))/dot_general | solution.py:56
  258.4 2.5 fusion.105
  260.9 2.6 fusion.75
  265.5 2.5 fusion.91
  268.0 4.4 fusion.38
  272.4 5.5 %fusion.97 = f32[4,4,64,64]{3,2,1,0:T(8,128)} fusion(f32[2,4,4,64,64]{4,3,2,1,0:T(8,128)S(1)} %fusion.38, f32[2,4,4,64,64]{4,3,2,1,0:T(8,128)S(1)} %fusion.347, f32[2,4,4,64,128]{4,3,2,1,0:T(8,128)S(1)} %fusion.91, f32[4,4,64,64]{3,2,1,0:T(8,128)S(1)} %mul.919, f32[64,64]{1,0:T(8,128)S(1)} %fusion.210, f32[2]{0:T(128)S(1)} %add_divide_fusion.6, ...), kind=kOutput, calls=%fused_computation.114 | convolution fusion | flops 202440704 | bytes 3998208 | tf_op jit(solution)/shard_map/transpose(jvp(...ab,kb->...ak))/dot_general | solution.py:47
  280.5 42.2 %all-reduce = f32[4,45,32]{1,0,2:T(4,128)S(1)} all-reduce(f32[4,45,32]{1,0,2:T(4,128)S(1)} %copy.194), channel_id=2, replica_groups=mesh['sub'=32] {'sub'}, use_global_device_ids=true, to_apply=%region_5.6.clone | all-reduce | flops 5760 | bytes 46080
  322.7 31.5 %all_gather.7 = f32[4,45,32]{1,0,2:T(4,128)S(1)} all-gather(f32[4,45,1]{1,0,2:T(4,128)S(1)} %fusion.212), channel_id=1, replica_groups=mesh['sub'=32] {'sub'}, dimensions={2}, use_global_device_ids=true | all-gather | bytes 23760 | tf_op jit(solution)/shard_map/all_gather | solution.py:114
  356.9 4.4 fusion.44
  361.3 5.1 %fusion.46 = f32[2,4,4,64,128]{4,3,2,1,0:T(8,128)S(1)} fusion(f32[4,4,64,64]{3,2,1,0:T(8,128)S(1)} %mul.967, f32[64,64]{1,0:T(8,128)S(1)} %fusion.210, f32[2]{0:T(128)S(1)} %add_divide_fusion.6, f32[128,128]{0,1:T(8,128)} %copy-done.11), kind=kOutput, calls=%fused_computation.80 | convolution fusion | flops 201588736 | bytes 1359880 | tf_op jit(solution)/shard_map/jvp(...ab,kb->...ak)/dot_general | solution.py:50
  366.4 4.7 fusion.69
  373.0 4.3 fusion.66
  383.1 2.5 fusion.6
  385.6 2.5 fusion.4
  394.5 2.7 subtract_reduce_fusion
  403.4 2.4 fusion.147
  407.9 3.6 fusion
  411.5 3.6 add_divide_fusion
  423.0 4.2 fusion.42
  427.3 5.7 %fusion.96 = f32[4,4,64,64]{3,2,1,0:T(8,128)} fusion(f32[2,4,4,64,64]{4,3,2,1,0:T(8,128)S(1)} %fusion.42, f32[2,4,4,64,64]{4,3,2,1,0:T(8,128)S(1)} %fusion.344, f32[2,4,4,64,128]{4,3,2,1,0:T(8,128)S(1)} %fusion.87, f32[4,4,64,64]{3,2,1,0:T(8,128)S(1)} %mul.967, f32[64,64]{1,0:T(8,128)S(1)} %fusion.210, f32[2]{0:T(128)S(1)} %add_divide_fusion.6, ...), kind=kOutput, calls=%fused_computation.113 | convolution fusion | flops 202440704 | bytes 3998208 | tf_op jit(solution)/shard_map/transpose(jvp(...ab,kb->...ak))/dot_general | solution.py:47
  435.6 49.2 %all-reduce.1 = f32[4,45,32]{1,0,2:T(4,128)S(1)} all-reduce(f32[4,45,32]{1,0,2:T(4,128)S(1)} %copy.224), channel_id=3, replica_groups=mesh['sub'=32] {'sub'}, use_global_device_ids=true, to_apply=%region_10.11.clone | all-reduce | flops 5760 | bytes 46080
  (99 shorter events, 71.0 us)
Async XLA Ops:
  0.6 106.8 %copy-start = (f32[45,4096]{1,0:T(8,128)S(1)}, f32[45,4096]{1,0:T(8,128)}, u32[]{:S(2)}) copy-start(f32[45,4096]{1,0:T(8,128)} %param.9) | copy-start | bytes 2211844
  30.1 6.1 %copy-start.15 = (f32[4,45,1]{1,2,0:T(1,128)S(1)}, f32[4,45,1]{1,2,0:T(1,128)}, u32[]{:S(2)}) copy-start(f32[4,45,1]{1,2,0:T(1,128)} %param.8) | copy-start | bytes 2164
  30.1 77.1 %copy-start.16 = (s32[4]{0:T(128)S(1)}, s32[4]{0:T(128)}, u32[]{:S(2)}) copy-start(s32[4]{0:T(128)} %param.7) | copy-start | bytes 52
  30.1 118.2 %all-to-all-start = ((f32[32,1,16384]{2,1,0:T(1,128)}), f32[32,1,16384]{2,1,0:T(1,128)}, u32[]{:S(2)}, u32[]{:S(2)}) async-start(f32[32,1,16384]{2,1,0:T(1,128)} %reshape.149), calls=%async_computation | async-start | bytes 4194304 | tf_op jit(solution)/shard_map/all_to_all | solution.py:68
  36.2 74.0 %copy-start.17 = (s32[4]{0:T(128)S(1)}, s32[4]{0:T(128)}, u32[]{:S(2)}) copy-start(s32[4]{0:T(128)} %param.6) | copy-start | bytes 52
  110.2 22.0 %copy-start.11 = (f32[128,128]{0,1:T(8,128)}, f32[128,128]{0,1:T(8,128)S(1)}, u32[]{:S(2)}) copy-start(f32[128,128]{0,1:T(8,128)S(1)} %fusion.194) | copy-start | bytes 196612
  139.5 61.6 %copy-start.4 = (f32[2,4,4,128,128]{4,3,2,1,0:T(8,128)}, f32[2,4,4,128,128]{4,3,2,1,0:T(8,128)S(1)}, u32[]{:S(2)}) copy-start(f32[2,4,4,128,128]{4,3,2,1,0:T(8,128)S(1)} %convolution_subtract_fusion.1) | copy-start | bytes 6291460
  143.0 1.3 copy-start.7
  186.0 26.8 %collective-permute-start = (f32[2,4,512,128]{3,2,1,0:T(8,128)}, f32[2,4,512,128]{3,2,1,0:T(8,128)}, u32[]{:S(2)}, u32[]{:S(2)}) collective-permute-start(f32[2,4,512,128]{3,2,1,0:T(8,128)} %bitcast.274), channel_id=1, source_target_pairs={{1,0},{2,1},{3,2},{4,3},{5,4},{6,5},{7,6},{8,7},{9,8},{10,9},{11,1... | collective-permute-start | bytes 6291464 | tf_op jit(solution)/shard_map/ppermute | solution.py:19
  197.3 3.8 copy-start.8
  205.7 2.1 copy-start.10
  207.7 2.1 copy-start.6
  215.5 1.7 copy-start.14
  231.1 2.0 copy-start.2
  253.4 4.9 %copy-start.1 = (f32[2,4,4,128,128]{3,4,2,1,0:T(8,128)S(1)}, f32[2,4,4,128,128]{3,4,2,1,0:T(8,128)}, u32[]{:S(2)}) copy-start(f32[2,4,4,128,128]{3,4,2,1,0:T(8,128)} %copy.193) | copy-start | bytes 6291460
  253.4 4.9 %copy-start.9 = (f32[2,4,4,128,128]{4,3,2,1,0:T(8,128)S(1)}, f32[2,4,4,128,128]{4,3,2,1,0:T(8,128)}, u32[]{:S(2)}) copy-start(f32[2,4,4,128,128]{4,3,2,1,0:T(8,128)} %copy-done.7) | copy-start | bytes 6291460
  253.4 4.9 %copy-start.12 = (f32[128,128]{0,1:T(8,128)S(1)}, f32[128,128]{0,1:T(8,128)}, u32[]{:S(2)}) copy-start(f32[128,128]{0,1:T(8,128)} %copy-done.11) | copy-start | bytes 196612
  258.4 2.5 copy-start.5
  356.9 9.5 %copy-start.13 = (f32[128,128]{0,1:T(8,128)S(1)}, f32[128,128]{0,1:T(8,128)}, u32[]{:S(2)}) copy-start(f32[128,128]{0,1:T(8,128)} %copy-done.11) | copy-start | bytes 196612
  392.2 2.3 copy-start.3
where the time goes:
time: 490 us; the launch traced here: 486 us
  blocking collectives  194 us (40%)
  matrix products  182 us (37%)
  local copies, waits for them, and re-layouts  70 us (14%)
  other arithmetic  18.1 us (4%)
  between operations  9.91 us (2%)
  starting transfers between devices  9.19 us (2%)
    all_gather x2, blocking collectives, on_device(): gathered = lax.all_gather(current, 'sub', axis=2, tiled=True)  102 us
    unnamed x2, blocking collectives  91.4 us
    unnamed x39, local copies, waits for them, and re-layouts  45.6 us
    dot_general x9, matrix products, complex_dft(): jnp.einsum('...ab,kb->...ak', real_part, right_real, precision=highest)  32.6 us
    dot_general x9, matrix products, complex_dft(): jnp.einsum('...ab,kb->...ak', real_part, right_imag, precision=highest)  28.1 us
    dot_general x9, matrix products, complex_dft(): jnp.einsum('ja,...ak->...jk', left_imag, half_real, precision=highest)  22.5 us
    dot_general x9, matrix products, complex_dft(): jnp.einsum('ja,...ak->...jk', left_real, half_imag, precision=highest)  21.8 us
    dot_general x9, matrix products, complex_dft(): jnp.einsum('ja,...ak->...jk', left_imag, half_imag, precision=highest)  21.1 us
  transfers between devices with their start and end apart: 2, of which 1 were waited for; matrix products, arithmetic and copies ran while one was open for 11% of the time, Pallas kernels for 0%

commit v1 on v0

--- a/solution.py
+++ b/solution.py
@@ -11,6 +11,27 @@
 PUP = 64
 GAMMA = 0.01
 STEP_SIZE = 0.05
+
+
+def laid_out(pieces, dim):
+    pieces = jnp.moveaxis(pieces, 0, dim)
+    shape = pieces.shape
+    return pieces.reshape(*shape[:dim], shape[dim] * shape[dim + 1], *shape[dim + 2 :])
+
+
+def grow_blocks(shard, axis):
+    length, index = (lax.axis_size(axis), lax.axis_index(axis))
+    parts, bit = (shard[None], 1)
+    while bit < length:
+        theirs = lax.ppermute(parts, axis, [(i, i ^ bit) for i in range(length)])
+        low = index & bit == 0
+        parts = jnp.concatenate([jnp.where(low, parts, theirs), jnp.where(low, theirs, parts)])
+        bit *= 2
+    return parts
+
+
+def doubled_up(x, axis, dim):
+    return laid_out(grow_blocks(x, axis), dim)
 
 
 def from_behind(block, axis, distance):
@@ -111,7 +132,7 @@
     current = coeffs
     gradient = jnp.zeros_like(coeffs)
     for iteration in range(ITERS):
-        gathered = lax.all_gather(current, "sub", axis=2, tiled=True)
+        gathered = doubled_up(current, "sub", 2)
         chosen = jnp.einsum("fmp,ps->fms", gathered, selector, precision=highest)
         loss_value, pullback = jax.vjp(objective, chosen)
         (slopes,) = pullback(jnp.ones_like(loss_value))

time: 490 us -> 435 us (0.89)
  blocking collectives: 194 us -> 83.9 us
  waiting for transfers between devices: 2.58 us -> 50.2 us
  starting transfers between devices: 9.19 us -> 20 us
    all_gather x2 -> x0, blocking collectives: 102 us -> none  [on_device(): gathered = lax.all_gather(current, 'sub', axis=2, tiled=True)]
    ppermute x0 -> x10, waiting for transfers between devices: none -> 42 us  [grow_blocks(): theirs = lax.ppermute(parts, axis, [(i, i ^ bit) for i in range(length)])]
    ppermute x0 -> x10, starting transfers between devices: none -> 11.2 us  [grow_blocks(): theirs = lax.ppermute(parts, axis, [(i, i ^ bit) for i in range(length)])]
    unnamed x2, blocking collectives: 91.4 us -> 83.9 us
    ppermute x1, waiting for transfers between devices: 2.58 us -> 8.17 us  [from_behind(): return lax.ppermute(block, axis, route)]
    unnamed x39 -> x35, local copies, waits for them, and re-layouts: 45.6 us -> 44.5 us
  transfers between devices with their start and end apart: 2 -> 12, of which waited for: 1 -> 10; matrix products, arithmetic and copies ran while one was open for 11% -> 12% of each run, Pallas kernels for 0% -> 0%
where the time goes in v1:
time: 435 us; the launch traced here: 429 us
  matrix products  181 us (42%)
  blocking collectives  83.9 us (19%)
  local copies, waits for them, and re-layouts  66.5 us (15%)
  waiting for transfers between devices  50.2 us (12%)
  starting transfers between devices  20 us (5%)
  other arithmetic  16.9 us (4%)
  between operations  9.97 us (2%)
    unnamed x2, blocking collectives  83.9 us
    unnamed x35, local copies, waits for them, and re-layouts  44.5 us
    ppermute x10, waiting for transfers between devices, grow_blocks(): theirs = lax.ppermute(parts, axis, [(i, i ^ bit) for i in range(length)])  42 us
    dot_general x9, matrix products, complex_dft(): jnp.einsum('...ab,kb->...ak', real_part, right_real, precision=highest)  32.6 us
    dot_general x9, matrix products, complex_dft(): jnp.einsum('...ab,kb->...ak', real_part, right_imag, precision=highest)  28.3 us
    dot_general x9, matrix products, complex_dft(): jnp.einsum('ja,...ak->...jk', left_imag, half_real, precision=highest)  24.1 us
    dot_general x9, matrix products, complex_dft(): jnp.einsum('ja,...ak->...jk', left_imag, half_imag, precision=highest)  21.1 us
    dot_general x9, matrix products, complex_dft(): jnp.einsum('ja,...ak->...jk', left_real, half_real, precision=highest)  20.2 us
  transfers between devices with their start and end apart: 12, of which 10 were waited for; matrix products, arithmetic and copies ran while one was open for 12% of the time, Pallas kernels for 0%

profile of v1, /device:TPU:10, one launch (start us, length us, event | category | flops | bytes accessed | tf_op | source)
XLA Modules:
  0.0 428.9 jit_solution(5118168849451816080)
XLA Ops:
  0.6 13.2 %copy.175 = f32[2,4,16,4096]{2,1,0,3:T(4,128)} copy(f32[2,4,16,4096]{3,2,1,0:T(8,128)} %param.5) | data formatting | bytes 4194304 | tf_op args[0]
  13.8 16.4 %reshape.157 = f32[32,1,16384]{2,1,0:T(1,128)} reshape(f32[4096,2,4,16]{3,2,1,0:T(4,128)} %bitcast.284) | data formatting | bytes 4194304
  30.2 6.2 %all-to-all-start = ((f32[32,1,16384]{2,1,0:T(1,128)}), f32[32,1,16384]{2,1,0:T(1,128)}, u32[]{:S(2)}, u32[]{:S(2)}) async-start(f32[32,1,16384]{2,1,0:T(1,128)} %reshape.157), calls=%async_computation | async-start | bytes 4194304 | tf_op jit(solution)/shard_map/all_to_all | solution.py:89
  38.8 9.4 %collective-permute-done.1 = f32[2,4,45,1]{2,0,1,3:T(2,128)S(1)} collective-permute-done((f32[2,4,45,1]{2,0,1,3:T(2,128)S(1)}, f32[2,4,45,1]{2,0,1,3:T(2,128)S(1)}, u32[]{:S(2)}, u32[]{:S(2)}) %collective-permute-start.1) | collective-permute-done | bytes 1472 | tf_op jit(solution)/shard_map/ppermute | solution.py:26
  52.0 3.0 collective-permute-start.3
  55.7 16.4 %collective-permute-done.3 = f32[8,4,45,1]{2,0,1,3:T(8,128)S(1)} collective-permute-done((f32[8,4,45,1]{2,0,1,3:T(8,128)S(1)}, f32[8,4,45,1]{2,0,1,3:T(8,128)S(1)}, u32[]{:S(2)}, u32[]{:S(2)}) %collective-permute-start.3) | collective-permute-done | bytes 5792 | tf_op jit(solution)/shard_map/ppermute | solution.py:26
  84.3 4.4 %fusion.52 = f32[2,4,4,64,128]{4,3,2,1,0:T(8,128)S(1)} fusion(f32[4,4,64,64]{3,2,1,0:T(8,128)S(1)} %mul.919, f32[64,64]{1,0:T(8,128)S(1)} %fusion.213, f32[2]{0:T(128)S(1)} %add_divide_fusion.6, f32[128,128]{0,1:T(8,128)S(1)} %sine_negate_fusion), kind=kOutput, calls=%fused_computation.83 | convolution fusion | flops 201588736 | bytes 1638912 | tf_op jit(solution)/shard_map/jvp(...ab,kb->...ak)/dot_general | solution.py:68
  88.7 4.4 %fusion.54 = f32[2,4,4,64,128]{4,3,2,1,0:T(8,128)S(1)} fusion(f32[4,4,64,64]{3,2,1,0:T(8,128)S(1)} %mul.919, f32[64,64]{1,0:T(8,128)S(1)} %fusion.213, f32[2]{0:T(128)S(1)} %add_divide_fusion.6, f32[128,128]{0,1:T(8,128)S(1)} %fusion.197), kind=kOutput, calls=%fused_computation.84 | convolution fusion | flops 201588736 | bytes 1638912 | tf_op jit(solution)/shard_map/jvp(...ab,kb->...ak)/dot_general | solution.py:71
  93.1 4.6 %fusion.63 = f32[2,4,4,64,128]{4,3,2,1,0:T(8,128)S(1)} fusion(f32[2,4,4,64,128]{4,3,2,1,0:T(8,128)S(1)} %fusion.52, f32[4,4,64,64]{3,2,1,0:T(8,128)S(1)} %mul.919, f32[64,64]{1,0:T(8,128)S(1)} %fusion.213, f32[2]{0:T(128)S(1)} %add_divide_fusion.6, f32[128,128]{0,1:T(8,128)S(1)} %fusion.197), kind=kOutput, calls=%fused_computation.88 | convolution fusion | flops 201850880 | bytes 2687488 | tf_op jit(solution)/shard_map/jvp(...ab,kb->...ak)/dot_general | solution.py:65
  97.7 4.4 %fusion.60 = f32[2,4,4,64,128]{4,3,2,1,0:T(8,128)S(1)} fusion(f32[2,4,4,64,128]{4,3,2,1,0:T(8,128)S(1)} %fusion.54, f32[4,4,64,64]{3,2,1,0:T(8,128)S(1)} %mul.919, f32[64,64]{1,0:T(8,128)S(1)} %fusion.213, f32[2]{0:T(128)S(1)} %add_divide_fusion.6, f32[128,128]{0,1:T(8,128)S(1)} %sine_negate_fusion), kind=kOutput, calls=%fused_computation.87 | convolution fusion | flops 201850880 | bytes 2687488 | tf_op jit(solution)/shard_map/jvp(...ab,kb->...ak)/dot_general | solution.py:66
  102.1 3.4 fusion.353
  105.6 3.9 fusion.354
  109.5 3.5 convolution_subtract_fusion.1
  113.0 4.8 %convolution_add_fusion.1 = f32[2,4,4,128,128]{4,3,2,1,0:T(8,128)} fusion(f32[2,4,4,128,128]{4,3,2,1,0:T(8,128)S(1)} %fusion.354, f32[2,4,4,64,128]{4,3,2,1,0:T(8,128)S(1)} %fusion.63, f32[128,128]{0,1:T(8,128)S(1)} %sine_negate_fusion), kind=kOutput, calls=%fused_computation.60 | convolution fusion | flops 403177472 | bytes 5275648 | tf_op jit(solution)/shard_map/jvp(ja,...ak->...jk)/dot_general | solution.py:77
  118.3 8.9 %reduce.6 = f32[32,16384]{1,0:T(8,128)} reduce(f32[32,1,16384]{2,1,0:T(1,128)} %all-to-all-done, f32[]{:T(128)} %broadcast.349), dimensions={1}, to_apply=%all_to_all.13.reduce_sub_computation | reduce | bytes 4194308 | tf_op jit(solution)/shard_map/all_to_all | solution.py:89
  127.2 14.7 %reshape.158 = f32[4096,2,4,16]{3,2,1,0:T(4,128)} reshape(f32[32,16384]{1,0:T(8,128)} %reduce.6) | data formatting | bytes 4194304
  141.9 13.7 %copy.288 = f32[2,4,16,32,128]{4,2,3,1,0:T(8,128)} copy(f32[2,4,16,32,128]{2,1,0,4,3:T(4,128)} %bitcast.283) | data formatting | bytes 4194304 | tf_op jit(solution)/shard_map/all_to_all | solution.py:89
  155.6 2.5 collective-permute-start.5
  158.1 4.1 fusion.14
  164.3 2.5 fusion.12
  173.8 8.2 %collective-permute-done.5 = f32[2,4,512,128]{3,2,1,0:T(8,128)S(1)} collective-permute-done((f32[2,4,512,128]{3,2,1,0:T(8,128)}, f32[2,4,512,128]{3,2,1,0:T(8,128)S(1)}, u32[]{:S(2)}, u32[]{:S(2)}) %collective-permute-start.5) | collective-permute-done | bytes 2097184 | tf_op jit(solution)/shard_map/ppermute | solution.py:40
  194.8 2.7 subtract_reduce_fusion.1
  207.9 3.6 fusion.8
  211.5 4.9 %add_divide_fusion.2 = f32[2,4,4,128,128]{4,3,2,1,0:T(8,128)} fusion(f32[2,4,4,128,128]{4,3,2,1,0:T(8,128)S(1)} %fusion.8, f32[2,4,4,128,128]{4,3,2,1,0:T(8,128)S(1)} %fusion.165, f32[2,4,4,128,128]{4,3,2,1,0:T(8,128)S(1)} %fusion.30, f32[]{:T(128)S(6)} %mul.931), kind=kOutput, calls=%fused_computation.48 | convolution fusion | flops 807124992 | bytes 8388612 | tf_op jit(solution)/shard_map/transpose(jvp(...ab,kb->...ak))/dot_general | solution.py:66
  216.5 3.4 copy.196
  219.9 4.9 %fusion.104 = f32[2,4,4,128,64]{3,4,2,1,0:T(8,128)S(1)} fusion(f32[2,4,4,128,128]{3,4,2,1,0:T(8,128)} %copy.196, f32[2,4,4,128,128]{4,3,2,1,0:T(8,128)} %convolution_add_fusion.1, f32[128,128]{0,1:T(8,128)S(1)} %sine_negate_fusion), kind=kOutput, calls=%fused_computation.125 | convolution fusion | flops 403701760 | bytes 5275648 | tf_op jit(solution)/shard_map/transpose(jvp(ja,...ak->...jk))/dot_general | solution.py:77
  224.8 2.5 fusion.105
  227.3 2.6 fusion.75
  231.9 2.5 fusion.91
  234.4 4.4 %fusion.38 = f32[2,4,4,64,64]{4,3,2,1,0:T(8,128)S(1)} fusion(f32[2,4,4,64,64]{4,3,2,1,0:T(8,128)S(1)} %fusion.348, f32[2,4,4,64,128]{4,3,2,1,0:T(8,128)S(1)} %fusion.91, f32[4,4,64,64]{3,2,1,0:T(8,128)S(1)} %mul.919, f32[64,64]{1,0:T(8,128)S(1)} %fusion.213, f32[2]{0:T(128)S(1)} %add_divide_fusion.6, f32[128,128]{0,1:T(8,128)S(1)} %copy-done.10), kind=kOutput, calls=%fused_computation.73 | convolution fusion | flops 201981952 | bytes 3211776 | tf_op jit(solution)/shard_map/transpose(jvp(...ab,kb->...ak))/dot_general | solution.py:65
  238.8 5.6 %fusion.97 = f32[4,4,64,64]{3,2,1,0:T(8,128)} fusion(f32[2,4,4,64,64]{4,3,2,1,0:T(8,128)S(1)} %fusion.38, f32[2,4,4,64,64]{4,3,2,1,0:T(8,128)S(1)} %fusion.352, f32[2,4,4,64,128]{4,3,2,1,0:T(8,128)S(1)} %fusion.91, f32[4,4,64,64]{3,2,1,0:T(8,128)S(1)} %mul.919, f32[64,64]{1,0:T(8,128)S(1)} %fusion.213, f32[2]{0:T(128)S(1)} %add_divide_fusion.6, ...), kind=kOutput, calls=%fused_computation.114 | convolution fusion | flops 202440704 | bytes 3998208 | tf_op jit(solution)/shard_map/transpose(jvp(...ab,kb->...ak))/dot_general | solution.py:68
  246.9 43.8 %all-reduce = f32[4,45,32]{1,0,2:T(4,128)S(1)} all-reduce(f32[4,45,32]{1,0,2:T(4,128)S(1)} %copy.197), channel_id=2, replica_groups=mesh['sub'=32] {'sub'}, use_global_device_ids=true, to_apply=%region_5.6.clone | all-reduce | flops 5760 | bytes 46080
  292.1 3.6 collective-permute-done.7
  300.4 3.0 collective-permute-done.9
  304.3 4.0 collective-permute-done.10
  311.0 4.4 %fusion.44 = f32[2,4,4,64,128]{4,3,2,1,0:T(8,128)S(1)} fusion(f32[4,4,64,64]{3,2,1,0:T(8,128)S(1)} %mul.967, f32[64,64]{1,0:T(8,128)S(1)} %fusion.213, f32[2]{0:T(128)S(1)} %add_divide_fusion.6, f32[128,128]{0,1:T(8,128)S(1)} %sine_negate_fusion), kind=kOutput, calls=%fused_computation.79 | convolution fusion | flops 201588736 | bytes 1638912 | tf_op jit(solution)/shard_map/jvp(...ab,kb->...ak)/dot_general | solution.py:68
  315.4 5.1 %fusion.46 = f32[2,4,4,64,128]{4,3,2,1,0:T(8,128)S(1)} fusion(f32[4,4,64,64]{3,2,1,0:T(8,128)S(1)} %mul.967, f32[64,64]{1,0:T(8,128)S(1)} %fusion.213, f32[2]{0:T(128)S(1)} %add_divide_fusion.6, f32[128,128]{0,1:T(8,128)} %copy-done.9), kind=kOutput, calls=%fused_computation.80 | convolution fusion | flops 201588736 | bytes 1359880 | tf_op jit(solution)/shard_map/jvp(...ab,kb->...ak)/dot_general | solution.py:71
  320.6 4.7 %fusion.69 = f32[2,4,4,64,128]{4,3,2,1,0:T(8,128)S(1)} fusion(f32[2,4,4,64,128]{4,3,2,1,0:T(8,128)S(1)} %fusion.44, f32[4,4,64,64]{3,2,1,0:T(8,128)S(1)} %mul.967, f32[64,64]{1,0:T(8,128)S(1)} %fusion.213, f32[2]{0:T(128)S(1)} %add_divide_fusion.6, f32[128,128]{0,1:T(8,128)S(1)} %copy-done.11), kind=kOutput, calls=%fused_computation.90 | convolution fusion | flops 201850880 | bytes 2687488 | tf_op jit(solution)/shard_map/jvp(...ab,kb->...ak)/dot_general | solution.py:65
  327.1 4.3 %fusion.66 = f32[2,4,4,64,128]{4,3,2,1,0:T(8,128)S(1)} fusion(f32[2,4,4,64,128]{4,3,2,1,0:T(8,128)S(1)} %fusion.46, f32[4,4,64,64]{3,2,1,0:T(8,128)S(1)} %mul.967, f32[64,64]{1,0:T(8,128)S(1)} %fusion.213, f32[2]{0:T(128)S(1)} %add_divide_fusion.6, f32[128,128]{0,1:T(8,128)S(1)} %sine_negate_fusion), kind=kOutput, calls=%fused_computation.89 | convolution fusion | flops 201850880 | bytes 2687488 | tf_op jit(solution)/shard_map/jvp(...ab,kb->...ak)/dot_general | solution.py:66
  337.2 2.5 fusion.6
  339.8 2.5 fusion.4
  348.7 2.7 subtract_reduce_fusion
  357.5 2.5 fusion.153
  362.1 3.6 fusion
  365.7 3.7 add_divide_fusion
  377.5 4.2 fusion.42
  381.7 4.7 %fusion.96 = f32[4,4,64,64]{3,2,1,0:T(8,128)S(1)} fusion(f32[2,4,4,64,64]{4,3,2,1,0:T(8,128)S(1)} %fusion.42, f32[2,4,4,64,64]{4,3,2,1,0:T(8,128)S(1)} %fusion.349, f32[2,4,4,64,128]{4,3,2,1,0:T(8,128)S(1)} %fusion.87, f32[4,4,64,64]{3,2,1,0:T(8,128)S(1)} %mul.967, f32[64,64]{1,0:T(8,128)S(1)} %fusion.213, f32[2]{0:T(128)S(1)} %add_divide_fusion.6, ...), kind=kOutput, calls=%fused_computation.113 | convolution fusion | flops 202440704 | bytes 3998208 | tf_op jit(solution)/shard_map/transpose(jvp(...ab,kb->...ak))/dot_general | solution.py:68
  387.9 40.1 %all-reduce.1 = f32[4,45,32]{1,0,2:T(4,128)S(1)} all-reduce(f32[4,45,32]{1,0,2:T(4,128)S(1)} %copy.226), channel_id=3, replica_groups=mesh['sub'=32] {'sub'}, use_global_device_ids=true, to_apply=%region_10.11.clone | all-reduce | flops 5760 | bytes 46080
  (131 shorter events, 89.5 us)
Async XLA Ops:
  0.6 82.9 %copy-start = (f32[45,4096]{1,0:T(8,128)S(1)}, f32[45,4096]{1,0:T(8,128)}, u32[]{:S(2)}) copy-start(f32[45,4096]{1,0:T(8,128)} %param.9) | copy-start | bytes 2211844
  30.2 6.3 %copy-start.13 = (f32[4,45,1]{1,2,0:T(1,128)S(1)}, f32[4,45,1]{1,2,0:T(1,128)}, u32[]{:S(2)}) copy-start(f32[4,45,1]{1,2,0:T(1,128)} %param.8) | copy-start | bytes 2164
  30.2 7.3 %copy-start.15 = (s32[4]{0:T(128)S(1)}, s32[4]{0:T(128)}, u32[]{:S(2)}) copy-start(s32[4]{0:T(128)} %param.6) | copy-start | bytes 52
  30.2 53.1 %copy-start.14 = (s32[4]{0:T(128)S(1)}, s32[4]{0:T(128)}, u32[]{:S(2)}) copy-start(s32[4]{0:T(128)} %param.7) | copy-start | bytes 52
  30.2 87.6 %all-to-all-start = ((f32[32,1,16384]{2,1,0:T(1,128)}), f32[32,1,16384]{2,1,0:T(1,128)}, u32[]{:S(2)}, u32[]{:S(2)}) async-start(f32[32,1,16384]{2,1,0:T(1,128)} %reshape.157), calls=%async_computation | async-start | bytes 4194304 | tf_op jit(solution)/shard_map/all_to_all | solution.py:89
  36.5 1.3 collective-permute-start
  37.8 10.3 %collective-permute-start.1 = (f32[2,4,45,1]{2,0,1,3:T(2,128)S(1)}, f32[2,4,45,1]{2,0,1,3:T(2,128)S(1)}, u32[]{:S(2)}, u32[]{:S(2)}) collective-permute-start(f32[2,4,45,1]{2,0,1,3:T(2,128)S(1)} %pad_maximum_fusion.6), channel_id=1, source_target_pairs={{0,2},{1,3},{2,0},{3,1},{4,6},{5,7},{6,4},{7,5},{8,10},{9,11},{10,... | collective-permute-start | bytes 4328 | tf_op jit(solution)/shard_map/ppermute | solution.py:26
  38.7 66.8 %copy-start.9 = (f32[128,128]{0,1:T(8,128)}, f32[128,128]{0,1:T(8,128)S(1)}, u32[]{:S(2)}) copy-start(f32[128,128]{0,1:T(8,128)S(1)} %fusion.197) | copy-start | bytes 196612
  48.2 3.7 collective-permute-start.2
  52.0 20.1 %collective-permute-start.3 = (f32[8,4,45,1]{2,0,1,3:T(8,128)S(1)}, f32[8,4,45,1]{2,0,1,3:T(8,128)S(1)}, u32[]{:S(2)}, u32[]{:S(2)}) collective-permute-start(f32[8,4,45,1]{2,0,1,3:T(8,128)S(1)} %pad_maximum_fusion.2), channel_id=1, source_target_pairs={{0,8},{1,9},{2,10},{3,11},{4,12},{5,13},{6,14},{7,15},{8,0},{9,1},... | collective-permute-start | bytes 17288 | tf_op jit(solution)/shard_map/ppermute | solution.py:26
  72.1 11.2 %collective-permute-start.4 = (f32[16,4,45,1]{2,0,1,3:T(8,128)S(1)}, f32[16,4,45,1]{2,0,1,3:T(8,128)S(1)}, u32[]{:S(2)}, u32[]{:S(2)}) collective-permute-start(f32[16,4,45,1]{2,0,1,3:T(8,128)S(1)} %pad_maximum_fusion), channel_id=1, source_target_pairs={{0,16},{1,17},{2,18},{3,19},{4,20},{5,21},{6,22},{7,23},{8,24},{9,... | collective-permute-start | bytes 34568 | tf_op jit(solution)/shard_map/ppermute | solution.py:26
  112.9 51.3 %copy-start.4 = (f32[2,4,4,128,128]{4,3,2,1,0:T(8,128)}, f32[2,4,4,128,128]{4,3,2,1,0:T(8,128)S(1)}, u32[]{:S(2)}) copy-start(f32[2,4,4,128,128]{4,3,2,1,0:T(8,128)S(1)} %convolution_subtract_fusion.1) | copy-start | bytes 6291460
  155.6 26.4 %collective-permute-start.5 = (f32[2,4,512,128]{3,2,1,0:T(8,128)}, f32[2,4,512,128]{3,2,1,0:T(8,128)S(1)}, u32[]{:S(2)}, u32[]{:S(2)}) collective-permute-start(f32[2,4,512,128]{3,2,1,0:T(8,128)} %bitcast.285), channel_id=1, source_target_pairs={{1,0},{2,1},{3,2},{4,3},{5,4},{6,5},{7,6},{8,7},{9,8},{10,9},{11,1... | collective-permute-start | bytes 6291464 | tf_op jit(solution)/shard_map/ppermute | solution.py:40
  162.2 2.1 copy-start.7
  170.9 2.5 copy-start.6
  182.9 0.8 copy-start.12
  197.5 2.0 copy-start.2
  219.8 4.9 %copy-start.1 = (f32[2,4,4,128,128]{3,4,2,1,0:T(8,128)S(1)}, f32[2,4,4,128,128]{3,4,2,1,0:T(8,128)}, u32[]{:S(2)}) copy-start(f32[2,4,4,128,128]{3,4,2,1,0:T(8,128)} %copy.196) | copy-start | bytes 6291460
  219.8 4.9 %copy-start.8 = (f32[2,4,4,128,128]{4,3,2,1,0:T(8,128)S(1)}, f32[2,4,4,128,128]{4,3,2,1,0:T(8,128)}, u32[]{:S(2)}) copy-start(f32[2,4,4,128,128]{4,3,2,1,0:T(8,128)} %convolution_add_fusion.1) | copy-start | bytes 6291460
  219.8 4.9 %copy-start.10 = (f32[128,128]{0,1:T(8,128)S(1)}, f32[128,128]{0,1:T(8,128)}, u32[]{:S(2)}) copy-start(f32[128,128]{0,1:T(8,128)} %copy-done.9) | copy-start | bytes 196612
  224.8 2.5 copy-start.5
  290.8 1.2 collective-permute-start.6
  292.0 3.7 collective-permute-start.7
  295.7 3.7 collective-permute-start.8
  299.5 4.0 collective-permute-start.9
  303.5 4.9 %collective-permute-start.10 = (f32[16,4,45,1]{2,0,1,3:T(8,128)S(1)}, f32[16,4,45,1]{2,0,1,3:T(8,128)S(1)}, u32[]{:S(2)}, u32[]{:S(2)}) collective-permute-start(f32[16,4,45,1]{2,0,1,3:T(8,128)S(1)} %pad_maximum_fusion.1), channel_id=1, source_target_pairs={{0,16},{1,17},{2,18},{3,19},{4,20},{5,21},{6,22},{7,23},{8,24},{9,... | collective-permute-start | bytes 34568 | tf_op jit(solution)/shard_map/ppermute | solution.py:26
  311.0 9.5 %copy-start.11 = (f32[128,128]{0,1:T(8,128)S(1)}, f32[128,128]{0,1:T(8,128)}, u32[]{:S(2)}) copy-start(f32[128,128]{0,1:T(8,128)} %copy-done.9) | copy-start | bytes 196612
  346.4 2.3 copy-start.3
